TPU v7x, 32 devices: a whole 2x2x4 slice. The times are simulated.
32 devices in a mesh: clip: 2 (over x), ord: 16 (over z, y, core).
Axes of the slice: x: 2, y: 2, z: 4, core: 2. Of those that a mesh axis runs over, the one named last changes fastest.
Arguments:
- reflection: bfloat16 [2, 16384, 8192], P(None, ('clip', 'ord')), parts along dimension 1, may hold values from -0.0625 to 0.0625
- incidence: bfloat16 [2, 8192, 16], replicated, may hold values from -6 to 6
- source_shift: int32 [16, 2], P('ord'), may hold values from -8 to 8
- source_weight: float32 [16], P('ord'), may hold values from 0.1 to 1
- grid_map: int32 [4096], replicated, may hold values from 0 to 4095, each once
- pupil_mask: int32 [64, 64], replicated, may hold values 0 or 1
- pupil_phase: float32 [2, 64, 64], replicated, may hold values from -3.140625 to 3.140625
- tile_order: int32 [16], replicated, may hold values from 0 to 15, each once
Outputs:
- aerial: float32 [2048, 2, 1024], P(('clip', 'ord')), parts along dimension 0
There are 2 independent parts, one for each index of `clip`. A program takes and returns all parts, laid end to end along the dimension named above; an argument that names none is the same for every part. Nothing has to cross between parts.
Inputs may be any that keep to these rules, and one draw needn't show every extreme that they name: `grid_map`: a permutation of the 4096 pupil cells. `tile_order`: a permutation of the 16 tiles.
All inputs are finite; a program needn't handle non-finite values.
Results may differ from a plain program's by a relative error of at most 0.0003.
Values may be sent and summed in bfloat16 or wider, within the bound.
A program may use at most 128 MiB of HBM per device.

v0:
```python
import math

import jax
import jax.numpy as jnp
from jax import lax
from jax.sharding import PartitionSpec as P

PIX = 1024


HIGHEST = lax.Precision.HIGHEST


def phase_table(left_ints, right_ints, period):
    turn_index = jnp.mod(left_ints[:, None] * right_ints[None, :], period).astype(jnp.float32)
    angles = turn_index * (2.0 * math.pi / period)
    return (jnp.cos(angles), jnp.sin(angles))


def band_kernel(points, period, grid_side):
    samples = 2 * grid_side
    difference = jnp.arange(1 - grid_side, grid_side, dtype=jnp.int32)
    fine_cos, fine_sin = phase_table(points, difference, period)
    coarse_cos, coarse_sin = phase_table(jnp.arange(samples, dtype=jnp.int32), difference, samples)
    joined = jnp.einsum("pm,cm->pc", fine_cos, coarse_cos, precision=HIGHEST)
    joined = joined + jnp.einsum("pm,cm->pc", fine_sin, coarse_sin, precision=HIGHEST)
    return joined / samples


def tile_lookup(row_index, tile_order, tile_rows):
    tile_number = row_index // tile_rows
    matches = tile_number[:, None] == jnp.arange(tile_order.shape[0], dtype=jnp.int32)[None, :]
    chosen = jnp.sum(jnp.where(matches, tile_order[None, :], 0), axis=1)
    return chosen * tile_rows + row_index % tile_rows


def pupil_amplitude(grid_cells, source_shift, pupil_mask, pupil_phase):
    grid_side = pupil_mask.shape[0]
    item_count = grid_cells.shape[0]
    margin = grid_side // 8
    cells_float = grid_cells.astype(jnp.float32).reshape(item_count, 2, 2, grid_side, grid_side)
    cell_real = cells_float[:, 0]
    cell_imag = cells_float[:, 1]
    open_pad = jnp.pad(pupil_mask.astype(jnp.float32), margin)
    phase_pad = jnp.pad(pupil_phase, ((0, 0), (margin, margin), (margin, margin)))

    def window(one_shift):
        row_start = margin + one_shift[0]
        col_start = margin + one_shift[1]
        opened = lax.dynamic_slice(open_pad, (row_start, col_start), (grid_side, grid_side))
        phased = lax.dynamic_slice(
            phase_pad, (jnp.zeros((), jnp.int32), row_start, col_start), (2, grid_side, grid_side)
        )
        return (opened, phased)

    opened, phased = jax.vmap(window)(source_shift)
    phase_cos = jnp.cos(phased)[:, :, None]
    phase_sin = jnp.sin(phased)[:, :, None]
    open_scale = opened[:, None, None] * (1.0 / math.sqrt(grid_side * grid_side))
    amp_real = (cell_real[:, None] * phase_cos - cell_imag[:, None] * phase_sin) * open_scale
    amp_imag = (cell_real[:, None] * phase_sin + cell_imag[:, None] * phase_cos) * open_scale
    return (amp_real, amp_imag)


def column_pass(amp_real, amp_imag, period, points):
    grid_side = amp_real.shape[-1]
    frequency = jnp.arange(grid_side, dtype=jnp.int32) - grid_side // 2
    cosine_table, sine_table = phase_table(frequency, points, period)
    rows_real = jnp.transpose(amp_real, (3, 0, 1, 2, 4)).reshape(-1, grid_side)
    rows_imag = jnp.transpose(amp_imag, (3, 0, 1, 2, 4)).reshape(-1, grid_side)
    stacked = jnp.concatenate([rows_real, rows_imag], 1)
    to_real = jnp.concatenate([cosine_table, -sine_table], 0)
    to_imag = jnp.concatenate([sine_table, cosine_table], 0)
    part_real = jnp.dot(stacked, to_real, precision=HIGHEST).reshape(grid_side, -1)
    part_imag = jnp.dot(stacked, to_imag, precision=HIGHEST).reshape(grid_side, -1)
    return jnp.concatenate([part_real, part_imag], 0)


def row_power(columns, row_points, period, weights):
    grid_side = columns.shape[0] // 2
    frequency = jnp.arange(grid_side, dtype=jnp.int32) - grid_side // 2
    cosine_table, sine_table = phase_table(row_points, frequency, period)
    row_lift = jnp.concatenate(
        [
            jnp.concatenate([cosine_table, -sine_table], 1),
            jnp.concatenate([sine_table, cosine_table], 1),
        ],
        0,
    )
    field_rows = jnp.dot(row_lift, columns, precision=HIGHEST)
    block_rows = row_points.shape[0]
    powers = (
        field_rows[:block_rows] * field_rows[:block_rows]
        + field_rows[block_rows:] * field_rows[block_rows:]
    )
    powers = powers.reshape(block_rows, weights.shape[0], 2, 2, -1)
    return jnp.einsum("bsfpx,s->bfx", powers, weights, precision=HIGHEST)


def local(
    reflection,
    incidence,
    source_shift,
    source_weight,
    grid_map,
    pupil_mask,
    pupil_phase,
    tile_order,
):
    devices = lax.axis_size("ord")
    local_rows = reflection.shape[1]
    source_count = source_shift.shape[0]
    grid_side = pupil_mask.shape[0]
    order_count = grid_side * grid_side
    pixels = PIX
    real_part = jnp.dot(reflection[0], incidence[0], preferred_element_type=jnp.float32) - jnp.dot(
        reflection[1], incidence[1], preferred_element_type=jnp.float32
    )
    imag_part = jnp.dot(reflection[0], incidence[1], preferred_element_type=jnp.float32) + jnp.dot(
        reflection[1], incidence[0], preferred_element_type=jnp.float32
    )
    fields = jnp.stack([real_part, imag_part]).astype(jnp.bfloat16)
    by_owner = fields.reshape(2, local_rows, devices, source_count)
    inverse = jnp.argsort(grid_map)
    received = lax.all_to_all(by_owner, "ord", split_axis=2, concat_axis=1, tiled=True)
    item_count = received.shape[3]
    ordered = jnp.take(received.reshape(2, 2, order_count, item_count), inverse, axis=2)
    grid_cells = jnp.transpose(ordered, (3, 0, 1, 2))
    amp_real, amp_imag = pupil_amplitude(grid_cells, source_shift, pupil_mask, pupil_phase)
    weights = source_weight / (source_count * devices)
    tile_rows = pixels // devices
    samples = 2 * grid_side
    sample_points = jnp.arange(samples, dtype=jnp.int32)
    columns = column_pass(amp_real, amp_imag, samples, sample_points)
    local_power = row_power(columns, sample_points, samples, weights)
    summed = lax.psum(local_power, "ord")
    row_index = lax.axis_index("ord") * tile_rows + jnp.arange(tile_rows, dtype=jnp.int32)
    image_rows = tile_lookup(row_index, tile_order, tile_rows)
    kernel_rows = band_kernel(image_rows, pixels, grid_side)
    kernel_cols = band_kernel(jnp.arange(pixels, dtype=jnp.int32), pixels, grid_side)
    partial_value = jnp.dot(kernel_rows, summed.reshape(samples, 2 * samples), precision=HIGHEST)
    partial_value = partial_value.reshape(tile_rows * 2, samples)
    aerial = jnp.einsum("rd,xd->rx", partial_value, kernel_cols, precision=HIGHEST).reshape(
        tile_rows, 2, pixels
    )
    return aerial


def solution(mesh):
    in_specs = (P(None, ("clip", "ord"), None), P(), P("ord", None), P("ord"), P(), P(), P(), P())
    out_specs = P(("clip", "ord"), None, None)
    return jax.shard_map(local, mesh=mesh, in_specs=in_specs, out_specs=out_specs, check_vma=False)
```

profile of v0, /device:TPU:0, one launch (start us, length us, event | category | flops | bytes accessed | tf_op | source)
XLA Modules:
  0.0 185.6 jit_solution(11292437768441231674)
XLA Ops:
  6.5 5.8 %fusion.2 = f32[512,16]{0,1:T(8,128)S(1)} fusion(bf16[2,512,8192]{2,1,0:T(8,128)(2,1)} %param.8, bf16[2,8192,16]{1,2,0:T(8,128)(2,1)} %param.9), kind=kOutput, calls=%fused_computation.3 | convolution fusion | flops 134217728 | bytes 8683520 | tf_op jit(solution)/shard_map/dot_general | solution.py:116
  12.3 6.5 %fusion = f32[512,16]{0,1:T(8,128)S(1)} fusion(bf16[2,512,8192]{2,1,0:T(8,128)(2,1)} %param.8, bf16[2,8192,16]{1,2,0:T(8,128)(2,1)} %param.9), kind=kOutput, calls=%fused_computation.1 | convolution fusion | flops 134217728 | bytes 8683520 | tf_op jit(solution)/shard_map/dot_general | solution.py:119
  18.9 2.3 %fusion.29 = bf16[1,512,16,1]{1,2,3,0:T(8,128)(2,1)S(1)} fusion(f32[512,16]{0,1:T(8,128)S(1)} %fusion.2, bf16[2,512,8192]{2,1,0:T(8,128)(2,1)S(1)} %copy-done.4, bf16[2,8192,16]{1,2,0:T(8,128)(2,1)S(1)} %copy-done.5), kind=kOutput, calls=%fused_computation.25 | convolution fusion | flops 134234112 | bytes 8699904 | tf_op jit(solution)/shard_map/dot_general | solution.py:116
  21.1 2.3 %fusion.32 = bf16[1,512,16,1]{1,2,3,0:T(8,128)(2,1)S(1)} fusion(f32[512,16]{0,1:T(8,128)S(1)} %fusion, bf16[2,512,8192]{2,1,0:T(8,128)(2,1)S(1)} %copy-done.4, bf16[2,8192,16]{1,2,0:T(8,128)(2,1)S(1)} %copy-done.5), kind=kOutput, calls=%fused_computation.26 | convolution fusion | flops 134234112 | bytes 8699904 | tf_op jit(solution)/shard_map/dot_general | solution.py:119
  23.4 0.7 copy.39
  24.1 7.4 %all-to-all-start = ((bf16[2,512,16,1]{1,0,3,2:T(2,128)(2,1)}), bf16[2,512,16,1]{1,0,3,2:T(2,128)(2,1)S(1)}, u32[]{:S(2)}, u32[]{:S(2)}) async-start(bf16[2,512,16,1]{1,0,3,2:T(2,128)(2,1)} %copy.39), calls=%async_computation | async-start | bytes 65536 | tf_op jit(solution)/shard_map/all_to_all | solution.py:125
  31.5 0.2 all-reduce.4.cloned.1.call-start
  31.7 0.6 fusion.151
  34.9 5.8 %sort.17 = (s32[4096]{0:T(1024)}, s32[4096]{0:T(1024)S(1)}) sort(s32[4096]{0:T(1024)S(1)} %copy-done.2, s32[4096]{0:T(1024)S(1)} %iota.72), dimensions={0}, to_apply=%region_1.2 | sort | flops 49152 | bytes 65536 | tf_op jit(solution)/shard_map/jit(argsort)/sort | solution.py:124
  40.7 0.2 fusion.117
  40.9 0.3 fusion.109
  41.2 0.5 fusion.86
  42.8 2.7 %fusion.39 = f32[1024,128]{1,0:T(8,128)S(1)} fusion(s32[127]{0:T(128)S(1)} %iota_add_fusion.1), kind=kOutput, calls=%fused_computation.34 | convolution fusion | flops 201801984 | bytes 524796 | tf_op jit(solution)/shard_map/pm,cm->pc/dot_general | solution.py:25
  45.5 0.6 fusion.103
  46.0 2.7 %fusion.14 = f32[1024,128,1]{1,0,2:T(8,128)S(1)} fusion(f32[1024,128]{1,0:T(8,128)S(1)} %fusion.39, s32[127]{0:T(128)S(1)} %iota_add_fusion.1), kind=kOutput, calls=%fused_computation.17 | convolution fusion | flops 202064128 | bytes 1049084 | tf_op jit(solution)/shard_map/pm,cm->pc/dot_general | solution.py:26
  48.9 4.1 %copy.41 = bf16[2,2,4096]{1,0,2:T(2,128)(2,1)} copy(bf16[2,2,4096]{2,1,0:T(2,128)(2,1)S(1)} %reshape.285) | data formatting | bytes 65536 | tf_op jit(solution)/shard_map/reshape | solution.py:127
  53.0 15.4 %gather_fusion = bf16[4096,2,2]{2,1,0:T(2,128)(2,1)S(1)} fusion(bf16[2,2,4096]{1,0,2:T(2,128)(2,1)} %copy.41, s32[4096]{0:T(1024)S(1)} %fusion.116), kind=kCustom, calls=%fused_computation | custom fusion | bytes 81920 | tf_op jit(solution)/shard_map/jit(_take)/gather | solution.py:127
  68.4 5.8 %fusion.12 = f32[1,2,2,64,64]{2,1,4,3,0:T(2,128)S(1)} fusion(bf16[1,2,2,64,64]{2,1,4,3,0:T(2,128)(2,1)S(1)} %bitcast.80, pred[64,64]{1,0:T(8,128)(4,1)S(1)} %broadcast_in_dim.32), kind=kLoop, calls=%fused_computation.14 | loop fusion | flops 32768 | bytes 102400 | tf_op jit(solution)/shard_map/convert_element_type | solution.py:41
  74.1 6.1 %fusion.150 = (f32[1,1,2,64,64]{2,1,4,3,0:T(1,128)}, f32[1,1,2,64,64]{2,1,4,3,0:T(1,128)S(1)}) fusion(f32[1,2,2,64,64]{2,1,4,3,0:T(2,128)S(1)} %fusion.12), kind=kLoop, calls=%fused_computation.173 | loop fusion | bytes 131072 | tf_op jit(solution)/shard_map/slice | solution.py:42
  80.2 2.3 %copy.42 = f32[2,64,64]{2,0,1:T(2,128)S(1)} copy(f32[2,64,64]{0,2,1:T(8,128)} %bitcast.79) | data formatting | bytes 65536 | tf_op jit(solution)/shard_map/mul | solution.py:60
  82.5 0.7 copy.44
  83.2 0.2 subtract_multiply_fusion
  83.4 0.3 fusion.72
  83.8 0.3 fusion.76
  84.1 0.6 fusion.45
  85.0 0.4 reduce_sum.19
  85.4 0.8 copy.48
  86.2 0.6 fusion.16
  86.7 89.1 %all-reduce.4.cloned.1.call-done = f32[2,128,128]{2,1,0:T(8,128)} async-done(((f32[2,128,128]{2,1,0:T(8,128)}), f32[2,128,128]{2,1,0:T(8,128)}) %all-reduce.4.cloned.1.call-update) | async-done | bytes 131088 | tf_op jit(solution)/shard_map/psum | solution.py:136
  175.8 1.2 fusion.152
  177.0 0.6 fusion.153
  177.6 1.2 copy.47
  (37 shorter events, 0.8 us)
Async XLA Ops:
  6.5 12.3 %copy-start.4 = (bf16[2,512,8192]{2,1,0:T(8,128)(2,1)S(1)}, bf16[2,512,8192]{2,1,0:T(8,128)(2,1)}, u32[]{:S(2)}) copy-start(bf16[2,512,8192]{2,1,0:T(8,128)(2,1)} %param.8) | copy-start | bytes 50331652
  6.5 12.3 %copy-start.5 = (bf16[2,8192,16]{1,2,0:T(8,128)(2,1)S(1)}, bf16[2,8192,16]{1,2,0:T(8,128)(2,1)}, u32[]{:S(2)}) copy-start(bf16[2,8192,16]{1,2,0:T(8,128)(2,1)} %param.9) | copy-start | bytes 1572868
  18.8 12.9 %copy-start.3 = (s32[1,2]{1,0:T(1,128)S(1)}, s32[1,2]{1,0:T(1,128)}, u32[]{:S(2)}) copy-start(s32[1,2]{1,0:T(1,128)} %param.10) | copy-start | bytes 28
  18.8 16.0 %copy-start.2 = (s32[4096]{0:T(1024)S(1)}, s32[4096]{0:T(1024)}, u32[]{:S(2)}) copy-start(s32[4096]{0:T(1024)} %param.12) | copy-start | bytes 49156
  18.8 22.4 %copy-start = (f32[2,64,64]{2,1,0:T(8,128)S(1)}, f32[2,64,64]{2,1,0:T(8,128)}, u32[]{:S(2)}) copy-start(f32[2,64,64]{2,1,0:T(8,128)} %param.14) | copy-start | bytes 98308
  21.1 20.7 %copy-start.1 = (s32[64,64]{1,0:T(8,128)S(1)}, s32[64,64]{1,0:T(8,128)}, u32[]{:S(2)}) copy-start(s32[64,64]{1,0:T(8,128)} %param.13) | copy-start | bytes 49156
  21.1 21.5 %copy-start.6 = (s32[16]{0:T(128)S(1)}, s32[16]{0:T(128)}, u32[]{:S(2)}) copy-start(s32[16]{0:T(128)} %param.15) | copy-start | bytes 196
  24.1 24.8 %all-to-all-start = ((bf16[2,512,16,1]{1,0,3,2:T(2,128)(2,1)}), bf16[2,512,16,1]{1,0,3,2:T(2,128)(2,1)S(1)}, u32[]{:S(2)}, u32[]{:S(2)}) async-start(bf16[2,512,16,1]{1,0,3,2:T(2,128)(2,1)} %copy.39), calls=%async_computation | async-start | bytes 65536 | tf_op jit(solution)/shard_map/all_to_all | solution.py:125
  31.5 144.3 %all-reduce.4.cloned.1.call-start = ((), (), s32[]{:S(2)}) async-start(), calls=%async_computation.1 | async-start | bytes 262144 | tf_op jit(solution)/shard_map/psum | solution.py:136
Sparse Core Ops, SparseCore 0:
  86.3 89.4 all-reduce.3
where the time goes:
time: 187 us; the launch traced here: 186 us
  waiting for transfers between devices  89.1 us (48%)
  local copies, waits for them, and re-layouts  32.8 us (18%)
  matrix products  26.4 us (14%)
  between operations  16.9 us (9%)
  other arithmetic  12.9 us (7%)
  starting transfers between devices  7.64 us (4%)
    psum x1, waiting for transfers between devices, local(): summed = lax.psum(local_power, 'ord')  89.1 us
    gather x1, local copies, waits for them, and re-layouts, local(): jnp.take(received.reshape(2, 2, order_count, item_count), inverse, axis=2)  15.4 us
    all_to_all x1, starting transfers between devices, local(): lax.all_to_all(by_owner, 'ord', split_axis=2, concat_axis=1, tiled=True)  7.41 us
    dot_general x1, matrix products, local(): jnp.dot(reflection[1], incidence[0], preferred_element_type=jnp.float32)  6.47 us
    slice x1, local copies, waits for them, and re-layouts, pupil_amplitude(): cell_real = cells_float[:, 0]  6.12 us
    dot_general x1, matrix products, local(): jnp.dot(reflection[1], incidence[1], preferred_element_type=jnp.float32)  5.79 us
    sort x1, other arithmetic, local(): inverse = jnp.argsort(grid_map)  5.77 us
    convert_element_type x1, other arithmetic, pupil_amplitude(): grid_cells.astype(jnp.float32)  5.76 us
  transfers between devices with their start and end apart: 2, of which 1 were waited for; matrix products, arithmetic and copies ran while one was open for 8% of the time, Pallas kernels for 0%

commit v1 on v0

v1 whole, which is shorter than its diff:
```python
import functools
import math

import jax
import jax.numpy as jnp
import numpy as np
from jax import lax
from jax.experimental import pallas as pl
from jax.experimental.pallas import tpu as pltpu
from jax.sharding import PartitionSpec as P

PIX = 1024
HIGHEST = lax.Precision.HIGHEST
NN = (((1,), (0,)), ((), ()))
NT = (((1,), (1,)), ((), ()))
MESH = pl.DeviceIdType.MESH


def turn_table(left, right, period):
    angles = np.mod(np.outer(left, right), period) * (2.0 * math.pi / period)
    return np.cos(angles), np.sin(angles)


def split_const(values):
    values = np.asarray(values, np.float32)
    high = values.astype(jnp.bfloat16)
    low = (values - high.astype(np.float32)).astype(jnp.bfloat16)
    return np.stack([high, low])


def lift_tables(grid_side):
    samples = 2 * grid_side
    frequency = np.arange(grid_side) - grid_side // 2
    cosine, sine = turn_table(frequency, np.arange(samples), samples)
    cols = np.block([[cosine, sine], [-sine, cosine]])
    rows = np.block([[cosine.T, -sine.T], [sine.T, cosine.T]])
    return split_const(cols), split_const(rows)


def band_table(pixels, grid_side):
    samples = 2 * grid_side
    difference = np.arange(1 - grid_side, grid_side)
    fine_cos, fine_sin = turn_table(np.arange(pixels), difference, pixels)
    coarse_cos, coarse_sin = turn_table(np.arange(samples), difference, samples)
    return split_const((fine_cos @ coarse_cos.T + fine_sin @ coarse_sin.T) / samples)


def split(values):
    high = values.astype(jnp.bfloat16)
    low = (values - high.astype(jnp.float32)).astype(jnp.bfloat16)
    return high, low


def dot3(left, right, dims):
    dot = functools.partial(lax.dot_general, dimension_numbers=dims, preferred_element_type=jnp.float32)
    return dot(left[0], right[0]) + (dot(left[0], right[1]) + dot(left[1], right[0]))


def optics_kernel(
    shift_ref,
    weight_ref,
    reflection_ref,
    incidence_ref,
    cells_ref,
    mask_ref,
    phase_ref,
    cols_ref,
    rows_ref,
    out_ref,
    refl_buf,
    inc_buf,
    acc_ref,
    send_buf,
    recv_buf,
    grid_acc,
    part_buf,
    gather_buf,
    load_sem,
    own_sem,
    a_send,
    a_recv,
    r_send,
    r_recv,
    g_send,
    g_recv,
    *,
    devices,
    chunks,
):
    me = lax.axis_index("ord")
    sources = inc_buf.shape[2]
    side = mask_ref.shape[0]
    samples = 2 * side
    depth = refl_buf.shape[2] // chunks

    def loads(c):
        span = pl.ds(c * depth, depth)
        return (
            pltpu.make_async_copy(incidence_ref.at[:, span, :], inc_buf.at[:, span, :], load_sem.at[0, c]),
            pltpu.make_async_copy(reflection_ref.at[:, :, span], refl_buf.at[:, :, span], load_sem.at[1, c]),
        )

    for c in range(chunks):
        for load in loads(c):
            load.start()

    barrier = pltpu.get_barrier_semaphore()

    def greet(j, carry):
        pl.semaphore_signal(barrier, inc=1, device_id={"ord": lax.rem(me + j, devices)}, device_id_type=MESH)
        return carry

    lax.fori_loop(1, devices, greet, 0)

    shift_y = shift_ref[0, 0]
    shift_x = shift_ref[0, 1]
    opened = mask_ref[...].astype(jnp.float32) * (1.0 / side)
    planes = []
    for f in range(2):
        planes += [jnp.cos(phase_ref[f]) * opened, jnp.sin(phase_ref[f]) * opened]
    row_at = lax.broadcasted_iota(jnp.int32, (side, side), 0)
    col_at = lax.broadcasted_iota(jnp.int32, (side, side), 1)
    pick_row = jnp.where(col_at == row_at + shift_y, 1.0, 0.0)
    from_at = lax.broadcasted_iota(jnp.int32, (side, 2 * side), 0)
    to_at = lax.broadcasted_iota(jnp.int32, (side, 2 * side), 1)
    half = jnp.where(to_at >= side, 1, 0)
    hit = from_at == to_at - half * side + shift_x
    pick_cos = jnp.where(hit, 1.0, 0.0)
    pick_sin = jnp.where(hit, jnp.where(half == 1, 1.0, -1.0), 0.0)
    windows = []
    for f in range(2):
        for kind, pick in ((0, pick_cos), (1, pick_sin)):
            moved = lax.dot_general(pick_row, planes[2 * f + kind], NN, precision=HIGHEST, preferred_element_type=jnp.float32)
            windows.append(lax.dot_general(moved, pick, NN, precision=HIGHEST, preferred_element_type=jnp.float32))

    for c in range(chunks):
        inc_load, refl_load = loads(c)
        span = pl.ds(c * depth, depth)
        inc_load.wait()
        first = inc_buf[0, span, :]
        second = inc_buf[1, span, :]
        join_a = jnp.concatenate([first, second], 1)
        join_b = jnp.concatenate([-second, first], 1)
        refl_load.wait()
        step = jnp.dot(refl_buf[0, :, span], join_a, preferred_element_type=jnp.float32)
        step = step + jnp.dot(refl_buf[1, :, span], join_b, preferred_element_type=jnp.float32)
        if c == 0:
            acc_ref[...] = step
        else:
            acc_ref[...] += step

    lanes = 2 * sources
    to_row = lax.broadcasted_iota(jnp.int32, (lanes, lanes), 0)
    from_col = lax.broadcasted_iota(jnp.int32, (lanes, lanes), 1)
    turned = jnp.where(from_col == to_row // 2 + (to_row % 2) * sources, 1.0, 0.0).astype(jnp.bfloat16)
    by_source = lax.dot_general(
        turned, acc_ref[...].astype(jnp.bfloat16), NT, preferred_element_type=jnp.float32
    )
    for s in range(sources):
        send_buf[s] = by_source[2 * s : 2 * s + 2].astype(jnp.bfloat16)

    pl.semaphore_wait(barrier, devices - 1)

    def fan(source_of, target, send_sem, recv_sem):
        def copy_to(peer, sender):
            return pltpu.make_async_remote_copy(
                src_ref=source_of(peer),
                dst_ref=target.at[sender],
                send_sem=send_sem.at[peer],
                recv_sem=recv_sem.at[sender],
                device_id={"ord": peer},
                device_id_type=MESH,
            )

        def start(j, carry):
            copy_to(lax.rem(me + j, devices), me).start()
            return carry

        def wait_recv(sender):
            copy_to(sender, sender).wait_recv()

        def drain(j, carry):
            copy_to(lax.rem(me + j, devices), me).wait_send()
            return carry

        return start, wait_recv, drain

    start, wait_recv, drain_a = fan(lambda d: send_buf.at[d], recv_buf, a_send, a_recv)
    own = pltpu.make_async_copy(send_buf.at[me], recv_buf.at[me], own_sem.at[0])
    own.start()
    lax.fori_loop(1, devices, start, 0)

    grid_acc[...] = jnp.zeros_like(grid_acc)
    local_rows = recv_buf.shape[2]
    per_pol = devices // 2
    cell_at = lax.broadcasted_iota(jnp.int32, (side, local_rows), 0)

    own.wait()

    def take(j, carry):
        r = lax.rem(me + j, devices)

        @pl.when(j > 0)
        def _():
            wait_recv(r)

        p = r // per_pol
        cells = cells_ref[lax.rem(r, per_pol)]
        cell_y = cells // side
        hit_y = jnp.where(cell_at == cell_y, 1.0, 0.0).astype(jnp.bfloat16)
        hit_x = cell_at == cells - cell_y * side
        values = recv_buf[r].astype(jnp.float32)
        spread = jnp.concatenate(
            [jnp.where(hit_x, values[0:1], 0.0), jnp.where(hit_x, values[1:2], 0.0)], 0
        ).astype(jnp.bfloat16)
        grid_acc[p] += lax.dot_general(hit_y, spread, NT, preferred_element_type=jnp.float32)
        return carry

    lax.fori_loop(0, devices, take, 0)

    amps = []
    for f in range(2):
        for p in range(2):
            cells = grid_acc[p]
            swapped = jnp.concatenate([cells[:, side:], cells[:, :side]], 1)
            amps.append(cells * windows[2 * f] + swapped * windows[2 * f + 1])
    stacked = split(jnp.concatenate(amps, 0))
    halves = dot3(stacked, (cols_ref[0], cols_ref[1]), NN)
    columns = jnp.concatenate(
        [
            jnp.concatenate(
                [
                    halves[i * side : (i + 1) * side, :samples],
                    halves[i * side : (i + 1) * side, samples:],
                ],
                0,
            )
            for i in range(4)
        ],
        1,
    )
    fields = dot3((rows_ref[0], rows_ref[1]), split(columns), NN)
    powers = fields[:samples] * fields[:samples] + fields[samples:] * fields[samples:]
    weight = weight_ref[0] * (1.0 / sources)
    summed = (
        jnp.concatenate(
            [
                powers[:, :samples] + powers[:, samples : 2 * samples],
                powers[:, 2 * samples : 3 * samples] + powers[:, 3 * samples :],
            ],
            1,
        )
        * weight
    )
    part_rows = part_buf.shape[1]
    part_buf[...] = summed.reshape(devices, part_rows, 2 * samples)

    start, wait_recv_r, drain_r = fan(lambda d: part_buf.at[d], gather_buf.at[0], r_send, r_recv)
    lax.fori_loop(1, devices, start, 0)

    def add(j, total):
        r = lax.rem(me + j, devices)
        wait_recv_r(r)
        return total + gather_buf[0, r]

    total = lax.fori_loop(1, devices, add, part_buf[me])
    gather_buf[1, me] = total

    start, wait_recv_g, drain_g = fan(lambda d: gather_buf.at[1, me], gather_buf.at[1], g_send, g_recv)
    lax.fori_loop(1, devices, start, 0)

    def arrive(j, carry):
        wait_recv_g(lax.rem(me + j, devices))
        return carry

    lax.fori_loop(1, devices, arrive, 0)
    out_ref[...] = gather_buf[1].reshape(samples, 2 * samples)
    lax.fori_loop(1, devices, drain_a, 0)
    lax.fori_loop(1, devices, drain_r, 0)
    lax.fori_loop(1, devices, drain_g, 0)


def image_kernel(tile_ref, rows_ref, cols_ref, samples_ref, out_ref):
    samples = cols_ref.shape[2]
    partial = dot3((rows_ref[0], rows_ref[1]), split(samples_ref[...]), NN)
    for f in range(2):
        piece = split(partial[:, f * samples : (f + 1) * samples])
        out_ref[:, f, :] = dot3(piece, (cols_ref[0], cols_ref[1]), NT)


def local(
    reflection,
    incidence,
    source_shift,
    source_weight,
    grid_map,
    pupil_mask,
    pupil_phase,
    tile_order,
):
    devices = lax.axis_size("ord")
    local_rows = reflection.shape[1]
    order2 = reflection.shape[2]
    sources = incidence.shape[2]
    side = pupil_mask.shape[0]
    samples = 2 * side
    assert source_shift.shape[0] == 1 and sources == devices
    chunks = 8
    cols, rows = lift_tables(side)
    table = band_table(PIX, side)
    vmem = pl.BlockSpec(memory_space=pltpu.VMEM)
    smem = pl.BlockSpec(memory_space=pltpu.SMEM)
    anywhere = pl.BlockSpec(memory_space=pl.ANY)
    part_rows = samples // devices
    dma = pltpu.SemaphoreType.DMA
    summed = pl.pallas_call(
        functools.partial(optics_kernel, devices=devices, chunks=chunks),
        out_shape=jax.ShapeDtypeStruct((samples, 2 * samples), jnp.float32),
        in_specs=[smem, smem, anywhere, anywhere, vmem, vmem, vmem, vmem, vmem],
        out_specs=vmem,
        scratch_shapes=[
            pltpu.VMEM((2, local_rows, order2), jnp.bfloat16),
            pltpu.VMEM((2, order2, sources), jnp.bfloat16),
            pltpu.VMEM((local_rows, 2 * sources), jnp.float32),
            pltpu.VMEM((devices, 2, local_rows), jnp.bfloat16),
            pltpu.VMEM((devices, 2, local_rows), jnp.bfloat16),
            pltpu.VMEM((2, side, samples), jnp.float32),
            pltpu.VMEM((devices, part_rows, 2 * samples), jnp.float32),
            pltpu.VMEM((2, devices, part_rows, 2 * samples), jnp.float32),
            dma((2, chunks)),
            dma((1,)),
            dma((devices,)),
            dma((devices,)),
            dma((devices,)),
            dma((devices,)),
            dma((devices,)),
            dma((devices,)),
        ],
        compiler_params=pltpu.CompilerParams(
            collective_id=0, has_side_effects=True, vmem_limit_bytes=48 * 1024 * 1024
        ),
    )(
        source_shift,
        source_weight,
        reflection,
        incidence,
        grid_map.reshape(devices // 2, 1, local_rows),
        pupil_mask,
        pupil_phase,
        jnp.asarray(cols),
        jnp.asarray(rows),
    )
    tile_rows = PIX // devices
    tile = lax.dynamic_slice(tile_order, (lax.axis_index("ord"),), (1,))
    return pl.pallas_call(
        image_kernel,
        out_shape=jax.ShapeDtypeStruct((tile_rows, 2, PIX), jnp.float32),
        grid_spec=pltpu.PrefetchScalarGridSpec(
            num_scalar_prefetch=1,
            grid=(1,),
            in_specs=[
                pl.BlockSpec((2, tile_rows, samples), lambda i, t: (0, t[0], 0)),
                pl.BlockSpec((2, PIX, samples), lambda i, t: (0, 0, 0)),
                pl.BlockSpec((samples, 2 * samples), lambda i, t: (0, 0)),
            ],
            out_specs=pl.BlockSpec((tile_rows, 2, PIX), lambda i, t: (0, 0, 0)),
        ),
    )(tile, jnp.asarray(table), jnp.asarray(table), summed)


def solution(mesh):
    in_specs = (P(None, ("clip", "ord"), None), P(), P("ord", None), P("ord"), P(), P(), P(), P())
    out_specs = P(("clip", "ord"), None, None)
    return jax.shard_map(local, mesh=mesh, in_specs=in_specs, out_specs=out_specs, check_vma=False)
```

time: 187 us -> 49.1 us (0.26)
  waiting for transfers between devices: 89.1 us -> 0 us
  Pallas kernels: 0 us -> 34.6 us
  matrix products: 26.4 us -> 0 us
  local copies, waits for them, and re-layouts: 32.8 us -> 13.3 us
  between operations: 16.9 us -> 0.68 us
  other arithmetic: 12.9 us -> 0 us
  starting transfers between devices: 7.64 us -> 0 us
    psum x1 -> x0, waiting for transfers between devices: 89.1 us -> none  [local(): summed = lax.psum(local_power, 'ord')]
    pallas_call x0 -> x2, Pallas kernels: none -> 34.6 us  [the longest x1 31.3 us: local(): pl.pallas_call(functools.partial(optics_kernel, devices=devices, chunks=c...]
    dot_general x13 -> x0, matrix products: 26.4 us -> none  [the longest x1 6.47 us: local(): jnp.dot(reflection[1], incidence[0], preferred_element_type=jnp.float32)]
    gather x1 -> x0, local copies, waits for them, and re-layouts: 15.4 us -> none  [local(): jnp.take(received.reshape(2, 2, order_count, item_count), inverse, axis=2)]
    unnamed x14 -> x17, local copies, waits for them, and re-layouts: 0.04 us -> 12.1 us
    all_to_all x1 -> x0, starting transfers between devices: 7.41 us -> none  [local(): lax.all_to_all(by_owner, 'ord', split_axis=2, concat_axis=1, tiled=True)]
    slice x2 -> x0, local copies, waits for them, and re-layouts: 6.73 us -> none  [the longest x1 6.12 us: pupil_amplitude(): cell_real = cells_float[:, 0]]
    convert_element_type x2 -> x0, other arithmetic: 5.77 us -> none  [the longest x1 5.76 us: pupil_amplitude(): grid_cells.astype(jnp.float32)]
  transfers between devices with their start and end apart: 2 -> 0, of which waited for: 1 -> 0; matrix products, arithmetic and copies ran while one was open for 8% -> 0% of each run, Pallas kernels for 0% -> 0%
where the time goes in v1:
time: 49.1 us; the launch traced here: 48.7 us
  Pallas kernels  34.6 us (70%)
  local copies, waits for them, and re-layouts  13.3 us (27%)
  between operations  0.68 us (1%)
    pallas_call x1, Pallas kernels, local(): pl.pallas_call(functools.partial(optics_kernel, devices=devices, chunks=c...  31.3 us
    unnamed x17, local copies, waits for them, and re-layouts  12.1 us
    pallas_call x1, Pallas kernels, local(): pl.pallas_call(image_kernel, out_shape=jax.ShapeDtypeStruct((tile_rows, 2...  3.35 us
    dynamic_slice x1, local copies, waits for them, and re-layouts, local(): tile = lax.dynamic_slice(tile_order, (lax.axis_index('ord'),), (1,))  1.27 us

profile of v1, /device:TPU:0, one launch (start us, length us, event | category | flops | bytes accessed | tf_op | source)
XLA Modules:
  0.0 48.7 jit_solution(11526538884602207686)
XLA Ops:
  0.7 1.3 %dynamic_slice.3.tile_ref = s32[1]{0:T(128)} dynamic-slice(s32[16]{0:T(128)} %param.18, s32[]{:T(128)S(6)} %select_n.3), dynamic_slice_sizes={1} | dynamic-slice | bytes 12 | tf_op jit(solution)/shard_map/dynamic_slice | solution.py:354
  1.9 4.5 %copy.12.incidence_ref = bf16[2,8192,16]{2,1,0:T(8,128)(2,1)} copy(bf16[2,8192,16]{1,2,0:T(8,128)(2,1)} %param.12) | data formatting | bytes 1048576 | tf_op args[1]
  6.4 0.0 copy-start
  6.4 2.2 %copy-done = bf16[2,8192,16]{2,1,0:T(8,128)(2,1)S(1)} copy-done((bf16[2,8192,16]{2,1,0:T(8,128)(2,1)S(1)}, bf16[2,8192,16]{2,1,0:T(8,128)(2,1)}, u32[]{:S(2)}) %copy-start) | copy-done | bytes 524312
  8.6 0.0 copy-start.2
  8.6 0.9 %copy-done.2 = bf16[2,256,128]{2,1,0:T(8,128)(2,1)S(1)} copy-done((bf16[2,256,128]{2,1,0:T(8,128)(2,1)S(1)}, bf16[2,256,128]{2,1,0:T(8,128)(2,1)}, u32[]{:S(2)}) %copy-start.2) | copy-done | bytes 131096
  9.5 0.0 copy-start.3
  9.5 0.9 %copy-done.3 = bf16[2,128,256]{2,1,0:T(8,128)(2,1)S(1)} copy-done((bf16[2,128,256]{2,1,0:T(8,128)(2,1)S(1)}, bf16[2,128,256]{2,1,0:T(8,128)(2,1)}, u32[]{:S(2)}) %copy-start.3) | copy-done | bytes 131096
  10.4 0.0 copy-start.4
  10.4 0.8 %copy-done.4 = f32[2,64,64]{2,1,0:T(8,128)S(1)} copy-done((f32[2,64,64]{2,1,0:T(8,128)S(1)}, f32[2,64,64]{2,1,0:T(8,128)}, u32[]{:S(2)}) %copy-start.4) | copy-done | bytes 32792
  11.2 0.0 copy-start.5
  11.2 0.8 %copy-done.5 = s32[64,64]{1,0:T(8,128)S(1)} copy-done((s32[64,64]{1,0:T(8,128)S(1)}, s32[64,64]{1,0:T(8,128)}, u32[]{:S(2)}) %copy-start.5) | copy-done | bytes 16408
  12.0 0.0 copy-start.6
  12.0 0.7 %copy-done.6 = s32[4096]{0:T(1024)S(1)} copy-done((s32[4096]{0:T(1024)S(1)}, s32[4096]{0:T(1024)}, u32[]{:S(2)}) %copy-start.6) | copy-done | bytes 16408
  12.7 0.0 copy-start.7
  12.7 0.7 %copy-done.7 = s32[1,2]{1,0:T(1,128)S(1)} copy-done((s32[1,2]{1,0:T(1,128)S(1)}, s32[1,2]{1,0:T(1,128)}, u32[]{:S(2)}) %copy-start.7) | copy-done | bytes 32
  13.4 31.3 %shard_map.109.samples_ref = f32[128,256]{1,0:T(8,128)S(1)} custom-call(s32[1,2]{1,0:T(1,128)S(1)} %copy-done.7, f32[1]{0:T(128)S(6)} %copy.13.weight_ref, bf16[2,512,8192]{2,1,0:T(8,128)(2,1)} %reflection_ref.1, bf16[2,8192,16]{2,1,0:T(8,128)(2,1)S(1)} %copy-done, s32[8,1,512]{2,1,0:T(1,128)S(1)} %bitcast.1, s32[64,64]{1,0:T(8,128)S(1)} %copy-done.5, ...), custom_call_target="tpu_custom_call" | custom-call | tf_op jit(solution)/shard_map/pallas_call | solution.py:316
  44.7 0.0 copy-start.1
  44.7 0.6 %copy-done.1 = f32[128,256]{1,0:T(8,128)} copy-done((f32[128,256]{1,0:T(8,128)}, f32[128,256]{1,0:T(8,128)S(1)}, u32[]{:S(2)}) %copy-start.1) | copy-done | bytes 131096
  45.3 3.4 %shard_map.110 = f32[64,2,1024]{2,1,0:T(2,128)} custom-call(s32[1]{0:T(128)} %dynamic_slice.3.tile_ref, bf16[2,1024,128]{2,1,0:T(8,128)(2,1)} %constant.16.clone.rows_ref.cols_ref, bf16[2,1024,128]{2,1,0:T(8,128)(2,1)} %constant.16.clone.rows_ref.cols_ref, f32[128,256]{1,0:T(8,128)} %copy-done.1), custom_call_target="tpu_custom_call" | custom-call | tf_op jit(solution)/shard_map/pallas_call | solution.py:355
Async XLA Ops:
  6.4 2.2 %copy-start = (bf16[2,8192,16]{2,1,0:T(8,128)(2,1)S(1)}, bf16[2,8192,16]{2,1,0:T(8,128)(2,1)}, u32[]{:S(2)}) copy-start(bf16[2,8192,16]{2,1,0:T(8,128)(2,1)} %copy.12.incidence_ref) | copy-start | bytes 1572868
  8.6 0.9 %copy-start.2 = (bf16[2,256,128]{2,1,0:T(8,128)(2,1)S(1)}, bf16[2,256,128]{2,1,0:T(8,128)(2,1)}, u32[]{:S(2)}) copy-start(bf16[2,256,128]{2,1,0:T(8,128)(2,1)} %constant.15.clone.rows_ref) | copy-start | bytes 393220
  9.5 0.9 %copy-start.3 = (bf16[2,128,256]{2,1,0:T(8,128)(2,1)S(1)}, bf16[2,128,256]{2,1,0:T(8,128)(2,1)}, u32[]{:S(2)}) copy-start(bf16[2,128,256]{2,1,0:T(8,128)(2,1)} %constant.14.clone.cols_ref) | copy-start | bytes 393220
  10.4 0.8 %copy-start.4 = (f32[2,64,64]{2,1,0:T(8,128)S(1)}, f32[2,64,64]{2,1,0:T(8,128)}, u32[]{:S(2)}) copy-start(f32[2,64,64]{2,1,0:T(8,128)} %phase_ref.1) | copy-start | bytes 98308
  11.2 0.8 %copy-start.5 = (s32[64,64]{1,0:T(8,128)S(1)}, s32[64,64]{1,0:T(8,128)}, u32[]{:S(2)}) copy-start(s32[64,64]{1,0:T(8,128)} %mask_ref.1) | copy-start | bytes 49156
  12.0 0.7 %copy-start.6 = (s32[4096]{0:T(1024)S(1)}, s32[4096]{0:T(1024)}, u32[]{:S(2)}) copy-start(s32[4096]{0:T(1024)} %param.15) | copy-start | bytes 49156
  12.7 0.7 %copy-start.7 = (s32[1,2]{1,0:T(1,128)S(1)}, s32[1,2]{1,0:T(1,128)}, u32[]{:S(2)}) copy-start(s32[1,2]{1,0:T(1,128)} %shift_ref.1) | copy-start | bytes 28
  44.7 0.7 %copy-start.1 = (f32[128,256]{1,0:T(8,128)}, f32[128,256]{1,0:T(8,128)S(1)}, u32[]{:S(2)}) copy-start(f32[128,256]{1,0:T(8,128)S(1)} %shard_map.109.samples_ref) | copy-start | bytes 393220

commit v2 on v1

--- a/solution.py
+++ b/solution.py
@@ -42,7 +42,7 @@
     difference = np.arange(1 - grid_side, grid_side)
     fine_cos, fine_sin = turn_table(np.arange(pixels), difference, pixels)
     coarse_cos, coarse_sin = turn_table(np.arange(samples), difference, samples)
-    return split_const((fine_cos @ coarse_cos.T + fine_sin @ coarse_sin.T) / samples)
+    return np.concatenate(split_const((fine_cos @ coarse_cos.T + fine_sin @ coarse_sin.T) / samples), 1)
 
 
 def split(values):
@@ -57,16 +57,30 @@
 
 
 def optics_kernel(
+    shift_hbm,
+    weight_hbm,
+    reflection_ref,
+    incidence_ref,
+    cells_hbm,
+    mask_hbm,
+    phase_hbm,
+    cols_hbm,
+    rows_hbm,
+    tile_hbm,
+    band_rows_hbm,
+    band_cols_hbm,
+    out_hbm,
     shift_ref,
     weight_ref,
-    reflection_ref,
-    incidence_ref,
     cells_ref,
     mask_ref,
     phase_ref,
     cols_ref,
     rows_ref,
-    out_ref,
+    tile_ref,
+    band_rows_ref,
+    band_cols_ref,
+    image_ref,
     refl_buf,
     inc_buf,
     acc_ref,
@@ -76,6 +90,7 @@
     part_buf,
     gather_buf,
     load_sem,
+    small_sem,
     own_sem,
     a_send,
     a_recv,
@@ -83,12 +98,13 @@
     r_recv,
     g_send,
     g_recv,
+    out_sem,
     *,
     devices,
     chunks,
 ):
     me = lax.axis_index("ord")
-    sources = inc_buf.shape[2]
+    sources = inc_buf.shape[1]
     side = mask_ref.shape[0]
     samples = 2 * side
     depth = refl_buf.shape[2] // chunks
@@ -96,13 +112,34 @@
     def loads(c):
         span = pl.ds(c * depth, depth)
         return (
-            pltpu.make_async_copy(incidence_ref.at[:, span, :], inc_buf.at[:, span, :], load_sem.at[0, c]),
+            pltpu.make_async_copy(incidence_ref.at[:, :, span], inc_buf.at[:, :, span], load_sem.at[0, c]),
             pltpu.make_async_copy(reflection_ref.at[:, :, span], refl_buf.at[:, :, span], load_sem.at[1, c]),
         )
 
+    smalls = [
+        pltpu.make_async_copy(source, target, small_sem.at[i])
+        for i, (source, target) in enumerate(
+            (
+                (shift_hbm, shift_ref),
+                (mask_hbm, mask_ref),
+                (phase_hbm, phase_ref),
+                (weight_hbm, weight_ref),
+                (cells_hbm, cells_ref),
+                (cols_hbm, cols_ref),
+                (rows_hbm, rows_ref),
+                (tile_hbm, tile_ref),
+                (band_rows_hbm, band_rows_ref),
+                (band_cols_hbm, band_cols_ref),
+            )
+        )
+    ]
+    for small in smalls[:3]:
+        small.start()
     for c in range(chunks):
         for load in loads(c):
             load.start()
+    for small in smalls[3:]:
+        small.start()
 
     barrier = pltpu.get_barrier_semaphore()
 
@@ -112,6 +149,8 @@
 
     lax.fori_loop(1, devices, greet, 0)
 
+    for small in smalls[:3]:
+        small.wait()
     shift_y = shift_ref[0, 0]
     shift_x = shift_ref[0, 1]
     opened = mask_ref[...].astype(jnp.float32) * (1.0 / side)
@@ -137,13 +176,13 @@
         inc_load, refl_load = loads(c)
         span = pl.ds(c * depth, depth)
         inc_load.wait()
-        first = inc_buf[0, span, :]
-        second = inc_buf[1, span, :]
-        join_a = jnp.concatenate([first, second], 1)
-        join_b = jnp.concatenate([-second, first], 1)
+        first = inc_buf[0, :, span]
+        second = inc_buf[1, :, span]
+        join_a = jnp.concatenate([first, second], 0)
+        join_b = jnp.concatenate([-second, first], 0)
         refl_load.wait()
-        step = jnp.dot(refl_buf[0, :, span], join_a, preferred_element_type=jnp.float32)
-        step = step + jnp.dot(refl_buf[1, :, span], join_b, preferred_element_type=jnp.float32)
+        step = lax.dot_general(refl_buf[0, :, span], join_a, NT, preferred_element_type=jnp.float32)
+        step = step + lax.dot_general(refl_buf[1, :, span], join_b, NT, preferred_element_type=jnp.float32)
         if c == 0:
             acc_ref[...] = step
         else:
@@ -186,6 +225,8 @@
         return start, wait_recv, drain
 
     start, wait_recv, drain_a = fan(lambda d: send_buf.at[d], recv_buf, a_send, a_recv)
+    for small in smalls[3:]:
+        small.wait()
     own = pltpu.make_async_copy(send_buf.at[me], recv_buf.at[me], own_sem.at[0])
     own.start()
     lax.fori_loop(1, devices, start, 0)
@@ -241,7 +282,7 @@
     )
     fields = dot3((rows_ref[0], rows_ref[1]), split(columns), NN)
     powers = fields[:samples] * fields[:samples] + fields[samples:] * fields[samples:]
-    weight = weight_ref[0] * (1.0 / sources)
+    weight = weight_ref[0, 0] * (1.0 / sources)
     summed = (
         jnp.concatenate(
             [
@@ -274,18 +315,31 @@
         return carry
 
     lax.fori_loop(1, devices, arrive, 0)
-    out_ref[...] = gather_buf[1].reshape(samples, 2 * samples)
+    tile_rows, _, pixels = image_ref.shape
+    pieces = out_sem.shape[0]
+    lift = band_rows_ref[tile_ref[me]]
+    high, low = split(gather_buf[1].reshape(samples, 2 * samples))
+    partial = jnp.dot(lift, jnp.concatenate([high, high], 0), preferred_element_type=jnp.float32)
+    partial = partial + jnp.dot(lift[:, :samples], low, preferred_element_type=jnp.float32)
+    high, low = split(jnp.concatenate([partial[:, :samples], partial[:, samples:]], 0))
+    twice = jnp.concatenate([high, high], 1)
+    width = pixels // pieces
+    stores = []
+    for i in range(pieces):
+        span = pl.ds(i * width, width)
+        table = band_cols_ref[span, :]
+        piece = lax.dot_general(twice, table, NT, preferred_element_type=jnp.float32)
+        piece = piece + lax.dot_general(low, table[:, :samples], NT, preferred_element_type=jnp.float32)
+        image_ref[:, 0, span] = piece[:tile_rows]
+        image_ref[:, 1, span] = piece[tile_rows:]
+        store = pltpu.make_async_copy(image_ref.at[:, :, span], out_hbm.at[:, :, span], out_sem.at[i])
+        store.start()
+        stores.append(store)
     lax.fori_loop(1, devices, drain_a, 0)
     lax.fori_loop(1, devices, drain_r, 0)
     lax.fori_loop(1, devices, drain_g, 0)
-
-
-def image_kernel(tile_ref, rows_ref, cols_ref, samples_ref, out_ref):
-    samples = cols_ref.shape[2]
-    partial = dot3((rows_ref[0], rows_ref[1]), split(samples_ref[...]), NN)
-    for f in range(2):
-        piece = split(partial[:, f * samples : (f + 1) * samples])
-        out_ref[:, f, :] = dot3(piece, (cols_ref[0], cols_ref[1]), NT)
+    for store in stores:
+        store.wait()
 
 
 def local(
@@ -308,19 +362,30 @@
     chunks = 8
     cols, rows = lift_tables(side)
     table = band_table(PIX, side)
-    vmem = pl.BlockSpec(memory_space=pltpu.VMEM)
-    smem = pl.BlockSpec(memory_space=pltpu.SMEM)
-    anywhere = pl.BlockSpec(memory_space=pl.ANY)
+    hbm = pl.BlockSpec(memory_space=pltpu.HBM)
     part_rows = samples // devices
     dma = pltpu.SemaphoreType.DMA
-    summed = pl.pallas_call(
+    tile_rows = PIX // devices
+    pieces = 4
+    return pl.pallas_call(
         functools.partial(optics_kernel, devices=devices, chunks=chunks),
-        out_shape=jax.ShapeDtypeStruct((samples, 2 * samples), jnp.float32),
-        in_specs=[smem, smem, anywhere, anywhere, vmem, vmem, vmem, vmem, vmem],
-        out_specs=vmem,
+        out_shape=jax.ShapeDtypeStruct((tile_rows, 2, PIX), jnp.float32),
+        in_specs=[hbm] * 12,
+        out_specs=hbm,
         scratch_shapes=[
+            pltpu.SMEM((1, 2), jnp.int32),
+            pltpu.SMEM((1, 1), jnp.float32),
+            pltpu.VMEM((devices // 2, 1, local_rows), jnp.int32),
+            pltpu.VMEM((side, side), jnp.int32),
+            pltpu.VMEM((2, side, side), jnp.float32),
+            pltpu.VMEM(cols.shape, jnp.bfloat16),
+            pltpu.VMEM(rows.shape, jnp.bfloat16),
+            pltpu.SMEM(tile_order.shape, jnp.int32),
+            pltpu.VMEM((devices, tile_rows, 2 * samples), jnp.bfloat16),
+            pltpu.VMEM(table.shape, jnp.bfloat16),
+            pltpu.VMEM((tile_rows, 2, PIX), jnp.float32),
             pltpu.VMEM((2, local_rows, order2), jnp.bfloat16),
-            pltpu.VMEM((2, order2, sources), jnp.bfloat16),
+            pltpu.VMEM((2, sources, order2), jnp.bfloat16),
             pltpu.VMEM((local_rows, 2 * sources), jnp.float32),
             pltpu.VMEM((devices, 2, local_rows), jnp.bfloat16),
             pltpu.VMEM((devices, 2, local_rows), jnp.bfloat16),
@@ -328,6 +393,7 @@
             pltpu.VMEM((devices, part_rows, 2 * samples), jnp.float32),
             pltpu.VMEM((2, devices, part_rows, 2 * samples), jnp.float32),
             dma((2, chunks)),
+            dma((10,)),
             dma((1,)),
             dma((devices,)),
             dma((devices,)),
@@ -335,37 +401,25 @@
             dma((devices,)),
             dma((devices,)),
             dma((devices,)),
+            dma((pieces,)),
         ],
         compiler_params=pltpu.CompilerParams(
-            collective_id=0, has_side_effects=True, vmem_limit_bytes=48 * 1024 * 1024
+            collective_id=0, has_side_effects=True, vmem_limit_bytes=67043328
         ),
     )(
         source_shift,
-        source_weight,
+        source_weight.reshape(1, 1),
         reflection,
-        incidence,
+        jnp.transpose(incidence, (0, 2, 1)),
         grid_map.reshape(devices // 2, 1, local_rows),
         pupil_mask,
         pupil_phase,
         jnp.asarray(cols),
         jnp.asarray(rows),
+        tile_order,
+        jnp.asarray(table.reshape(devices, tile_rows, 2 * samples)),
+        jnp.asarray(table),
     )
-    tile_rows = PIX // devices
-    tile = lax.dynamic_slice(tile_order, (lax.axis_index("ord"),), (1,))
-    return pl.pallas_call(
-        image_kernel,
-        out_shape=jax.ShapeDtypeStruct((tile_rows, 2, PIX), jnp.float32),
-        grid_spec=pltpu.PrefetchScalarGridSpec(
-            num_scalar_prefetch=1,
-            grid=(1,),
-            in_specs=[
-                pl.BlockSpec((2, tile_rows, samples), lambda i, t: (0, t[0], 0)),
-                pl.BlockSpec((2, PIX, samples), lambda i, t: (0, 0, 0)),
-                pl.BlockSpec((samples, 2 * samples), lambda i, t: (0, 0)),
-            ],
-            out_specs=pl.BlockSpec((tile_rows, 2, PIX), lambda i, t: (0, 0, 0)),
-        ),
-    )(tile, jnp.asarray(table), jnp.asarray(table), summed)
 
 
 def solution(mesh):

time: 49.1 us -> 35.4 us (0.72)
  local copies, waits for them, and re-layouts: 13.3 us -> 1.87 us
  Pallas kernels: 34.6 us -> 32.7 us
    unnamed x17 -> x1, local copies, waits for them, and re-layouts: 12.1 us -> 1.87 us
    pallas_call x1 -> x0, Pallas kernels: 3.35 us -> none  [local(): pl.pallas_call(image_kernel, out_shape=jax.ShapeDtypeStruct((tile_rows, 2...]
    pallas_call x1, Pallas kernels: 31.3 us -> 32.7 us  [local(): pl.pallas_call(functools.partial(optics_kernel, devices=devices, chunks=c...]
    dynamic_slice x1 -> x0, local copies, waits for them, and re-layouts: 1.27 us -> none  [local(): tile = lax.dynamic_slice(tile_order, (lax.axis_index('ord'),), (1,))]
where the time goes in v2:
time: 35.4 us; the launch traced here: 35.2 us
  Pallas kernels  32.7 us (92%)
  local copies, waits for them, and re-layouts  1.87 us (5%)
  between operations  0.66 us (2%)
    pallas_call x1, Pallas kernels, local(): pl.pallas_call(functools.partial(optics_kernel, devices=devices, chunks=c...  32.7 us
    unnamed x1, local copies, waits for them, and re-layouts  1.87 us

profile of v2, /device:TPU:0, one launch (start us, length us, event | category | flops | bytes accessed | tf_op | source)
XLA Modules:
  0.0 35.2 jit_solution(2033281914730260646)
XLA Ops:
  0.7 32.7 %shard_map.118 = f32[64,2,1024]{2,1,0:T(2,128)} custom-call(s32[1,2]{1,0:T(1,128)} %shift_hbm.1, f32[1,1]{1,0:T(1,128)} %bitcast.3.weight_hbm, bf16[2,512,8192]{2,1,0:T(8,128)(2,1)} %reflection_ref.1, bf16[2,16,8192]{2,1,0:T(8,128)(2,1)} %bitcast.4, s32[8,1,512]{2,1,0:T(1,128)} %bitcast.5, s32[64,64]{1,0:T(8,128)} %mask_hbm.1, f32[2,64,64]{2,1,0:T(8,128)} %phase_hbm.1, ...), custom_call_target="tpu_custom_call" | custom-call | tf_op jit(solution)/shard_map/pallas_call | solution.py:370
  33.3 1.9 %copy.15 = f32[64,2,1024]{2,1,0:T(2,128)} copy(f32[64,2,1024]{2,1,0:T(2,128)} %shard_map.118) | data formatting | bytes 1048576

commit v3 on v2

--- a/solution.py
+++ b/solution.py
@@ -86,7 +86,7 @@
     acc_ref,
     send_buf,
     recv_buf,
-    grid_acc,
+    hit_ref,
     part_buf,
     gather_buf,
     load_sem,
@@ -133,12 +133,10 @@
             )
         )
     ]
-    for small in smalls[:3]:
-        small.start()
     for c in range(chunks):
         for load in loads(c):
             load.start()
-    for small in smalls[3:]:
+    for small in smalls:
         small.start()
 
     barrier = pltpu.get_barrier_semaphore()
@@ -149,7 +147,64 @@
 
     lax.fori_loop(1, devices, greet, 0)
 
-    for small in smalls[:3]:
+    for c in range(chunks):
+        inc_load, refl_load = loads(c)
+        span = pl.ds(c * depth, depth)
+        inc_load.wait()
+        first = inc_buf[0, :, span]
+        second = inc_buf[1, :, span]
+        join_a = jnp.concatenate([first, second], 0)
+        join_b = jnp.concatenate([-second, first], 0)
+        refl_load.wait()
+        step = lax.dot_general(join_a, refl_buf[0, :, span], NT, preferred_element_type=jnp.float32)
+        step = step + lax.dot_general(join_b, refl_buf[1, :, span], NT, preferred_element_type=jnp.float32)
+        if c == 0:
+            acc_ref[...] = step
+        else:
+            acc_ref[...] += step
+
+    lanes = 2 * sources
+    to_row = lax.broadcasted_iota(jnp.int32, (lanes, lanes), 0)
+    from_col = lax.broadcasted_iota(jnp.int32, (lanes, lanes), 1)
+    turned = jnp.where(from_col == to_row // 2 + (to_row % 2) * sources, 1.0, 0.0).astype(jnp.bfloat16)
+    by_source = lax.dot_general(
+        turned, acc_ref[...].astype(jnp.bfloat16), NN, preferred_element_type=jnp.float32
+    )
+    for s in range(sources):
+        send_buf[s] = by_source[2 * s : 2 * s + 2].astype(jnp.bfloat16)
+
+    pl.semaphore_wait(barrier, devices - 1)
+
+    def fan(source_of, target, send_sem, recv_sem):
+        def copy_to(peer, sender):
+            return pltpu.make_async_remote_copy(
+                src_ref=source_of(peer),
+                dst_ref=target.at[sender],
+                send_sem=send_sem.at[peer],
+                recv_sem=recv_sem.at[sender],
+                device_id={"ord": peer},
+                device_id_type=MESH,
+            )
+
+        def start(j, carry):
+            copy_to(lax.rem(me + j, devices), me).start()
+            return carry
+
+        def wait_recv(sender):
+            copy_to(sender, sender).wait_recv()
+
+        def drain(j, carry):
+            copy_to(lax.rem(me + j, devices), me).wait_send()
+            return carry
+
+        return start, wait_recv, drain
+
+    start, wait_recv, drain_a = fan(lambda d: send_buf.at[d], recv_buf, a_send, a_recv)
+    own = pltpu.make_async_copy(send_buf.at[me], recv_buf.at[me], own_sem.at[0])
+    own.start()
+    lax.fori_loop(1, devices, start, 0)
+
+    for small in smalls:
         small.wait()
     shift_y = shift_ref[0, 0]
     shift_x = shift_ref[0, 1]
@@ -172,97 +227,38 @@
             moved = lax.dot_general(pick_row, planes[2 * f + kind], NN, precision=HIGHEST, preferred_element_type=jnp.float32)
             windows.append(lax.dot_general(moved, pick, NN, precision=HIGHEST, preferred_element_type=jnp.float32))
 
-    for c in range(chunks):
-        inc_load, refl_load = loads(c)
-        span = pl.ds(c * depth, depth)
-        inc_load.wait()
-        first = inc_buf[0, :, span]
-        second = inc_buf[1, :, span]
-        join_a = jnp.concatenate([first, second], 0)
-        join_b = jnp.concatenate([-second, first], 0)
-        refl_load.wait()
-        step = lax.dot_general(refl_buf[0, :, span], join_a, NT, preferred_element_type=jnp.float32)
-        step = step + lax.dot_general(refl_buf[1, :, span], join_b, NT, preferred_element_type=jnp.float32)
-        if c == 0:
-            acc_ref[...] = step
-        else:
-            acc_ref[...] += step
-
-    lanes = 2 * sources
-    to_row = lax.broadcasted_iota(jnp.int32, (lanes, lanes), 0)
-    from_col = lax.broadcasted_iota(jnp.int32, (lanes, lanes), 1)
-    turned = jnp.where(from_col == to_row // 2 + (to_row % 2) * sources, 1.0, 0.0).astype(jnp.bfloat16)
-    by_source = lax.dot_general(
-        turned, acc_ref[...].astype(jnp.bfloat16), NT, preferred_element_type=jnp.float32
-    )
-    for s in range(sources):
-        send_buf[s] = by_source[2 * s : 2 * s + 2].astype(jnp.bfloat16)
-
-    pl.semaphore_wait(barrier, devices - 1)
-
-    def fan(source_of, target, send_sem, recv_sem):
-        def copy_to(peer, sender):
-            return pltpu.make_async_remote_copy(
-                src_ref=source_of(peer),
-                dst_ref=target.at[sender],
-                send_sem=send_sem.at[peer],
-                recv_sem=recv_sem.at[sender],
-                device_id={"ord": peer},
-                device_id_type=MESH,
-            )
-
-        def start(j, carry):
-            copy_to(lax.rem(me + j, devices), me).start()
-            return carry
-
-        def wait_recv(sender):
-            copy_to(sender, sender).wait_recv()
-
-        def drain(j, carry):
-            copy_to(lax.rem(me + j, devices), me).wait_send()
-            return carry
-
-        return start, wait_recv, drain
-
-    start, wait_recv, drain_a = fan(lambda d: send_buf.at[d], recv_buf, a_send, a_recv)
-    for small in smalls[3:]:
-        small.wait()
-    own = pltpu.make_async_copy(send_buf.at[me], recv_buf.at[me], own_sem.at[0])
-    own.start()
-    lax.fori_loop(1, devices, start, 0)
-
-    grid_acc[...] = jnp.zeros_like(grid_acc)
+
     local_rows = recv_buf.shape[2]
     per_pol = devices // 2
     cell_at = lax.broadcasted_iota(jnp.int32, (side, local_rows), 0)
-
+    for q in range(per_pol):
+        cells = cells_ref[q]
+        cell_y = cells // side
+        hit_ref[q, 0] = jnp.where(cell_at == cell_y, 1.0, 0.0).astype(jnp.bfloat16)
+        hit_ref[q, 1] = jnp.where(cell_at == cells - cell_y * side, 1.0, 0.0).astype(jnp.bfloat16)
+
+    def take(j, carry):
+        wait_recv(lax.rem(me + j, devices))
+        return carry
+
+    lax.fori_loop(1, devices, take, 0)
     own.wait()
-
-    def take(j, carry):
-        r = lax.rem(me + j, devices)
-
-        @pl.when(j > 0)
-        def _():
-            wait_recv(r)
-
-        p = r // per_pol
-        cells = cells_ref[lax.rem(r, per_pol)]
-        cell_y = cells // side
-        hit_y = jnp.where(cell_at == cell_y, 1.0, 0.0).astype(jnp.bfloat16)
-        hit_x = cell_at == cells - cell_y * side
-        values = recv_buf[r].astype(jnp.float32)
-        spread = jnp.concatenate(
-            [jnp.where(hit_x, values[0:1], 0.0), jnp.where(hit_x, values[1:2], 0.0)], 0
-        ).astype(jnp.bfloat16)
-        grid_acc[p] += lax.dot_general(hit_y, spread, NT, preferred_element_type=jnp.float32)
-        return carry
-
-    lax.fori_loop(0, devices, take, 0)
+    grid = None
+    for q in range(per_pol):
+        hit_x = hit_ref[q, 1]
+        spread = []
+        for p in range(2):
+            values = recv_buf[p * per_pol + q]
+            spread += [hit_x * values[0:1], hit_x * values[1:2]]
+        term = lax.dot_general(
+            hit_ref[q, 0], jnp.concatenate(spread, 0), NT, preferred_element_type=jnp.float32
+        )
+        grid = term if grid is None else grid + term
 
     amps = []
     for f in range(2):
         for p in range(2):
-            cells = grid_acc[p]
+            cells = grid[:, p * samples : (p + 1) * samples]
             swapped = jnp.concatenate([cells[:, side:], cells[:, :side]], 1)
             amps.append(cells * windows[2 * f] + swapped * windows[2 * f + 1])
     stacked = split(jnp.concatenate(amps, 0))
@@ -359,7 +355,7 @@
     side = pupil_mask.shape[0]
     samples = 2 * side
     assert source_shift.shape[0] == 1 and sources == devices
-    chunks = 8
+    chunks = 16
     cols, rows = lift_tables(side)
     table = band_table(PIX, side)
     hbm = pl.BlockSpec(memory_space=pltpu.HBM)
@@ -386,10 +382,10 @@
             pltpu.VMEM((tile_rows, 2, PIX), jnp.float32),
             pltpu.VMEM((2, local_rows, order2), jnp.bfloat16),
             pltpu.VMEM((2, sources, order2), jnp.bfloat16),
-            pltpu.VMEM((local_rows, 2 * sources), jnp.float32),
+            pltpu.VMEM((2 * sources, local_rows), jnp.float32),
             pltpu.VMEM((devices, 2, local_rows), jnp.bfloat16),
             pltpu.VMEM((devices, 2, local_rows), jnp.bfloat16),
-            pltpu.VMEM((2, side, samples), jnp.float32),
+            pltpu.VMEM((devices // 2, 2, side, local_rows), jnp.bfloat16),
             pltpu.VMEM((devices, part_rows, 2 * samples), jnp.float32),
             pltpu.VMEM((2, devices, part_rows, 2 * samples), jnp.float32),
             dma((2, chunks)),

time: 35.4 us -> 31.7 us (0.90)
  Pallas kernels: 32.7 us -> 29 us
    pallas_call x1, Pallas kernels: 32.7 us -> 29 us  [local(): pl.pallas_call(functools.partial(optics_kernel, devices=devices, chunks=c...]
where the time goes in v3:
time: 31.7 us; the launch traced here: 31.5 us
  Pallas kernels  29 us (91%)
  local copies, waits for them, and re-layouts  1.87 us (6%)
  between operations  0.66 us (2%)
    pallas_call x1, Pallas kernels, local(): pl.pallas_call(functools.partial(optics_kernel, devices=devices, chunks=c...  29 us
    unnamed x1, local copies, waits for them, and re-layouts  1.87 us

profile of v3, /device:TPU:0, one launch (start us, length us, event | category | flops | bytes accessed | tf_op | source)
XLA Modules:
  0.0 31.5 jit_solution(17830856753498372425)
XLA Ops:
  0.7 29.0 %shard_map.118 = f32[64,2,1024]{2,1,0:T(2,128)} custom-call(s32[1,2]{1,0:T(1,128)} %shift_hbm.1, f32[1,1]{1,0:T(1,128)} %bitcast.3.weight_hbm, bf16[2,512,8192]{2,1,0:T(8,128)(2,1)} %reflection_ref.1, bf16[2,16,8192]{2,1,0:T(8,128)(2,1)} %bitcast.4, s32[8,1,512]{2,1,0:T(1,128)} %bitcast.5, s32[64,64]{1,0:T(8,128)} %mask_hbm.1, f32[2,64,64]{2,1,0:T(8,128)} %phase_hbm.1, ...), custom_call_target="tpu_custom_call" | custom-call | tf_op jit(solution)/shard_map/pallas_call | solution.py:366
  29.7 1.9 %copy.15 = f32[64,2,1024]{2,1,0:T(2,128)} copy(f32[64,2,1024]{2,1,0:T(2,128)} %shard_map.118) | data formatting | bytes 1048576
